TPU v7x, 32 devices: a whole 2x2x4 slice. The times are simulated.
32 devices in a mesh: dp: 16 (over z, y, core), ctx: 2 (over x).
Axes of the slice: x: 2, y: 2, z: 4, core: 2. Of those that a mesh axis runs over, the one named last changes fastest.
Arguments:
- tokens: bfloat16 [32, 1024, 768], P('dp', 'ctx'), may hold values from -17 to 17
- segments: int32 [32, 1024], P('dp'), may hold values from 0 to 7, never falling along the last dimension, each value on 1 to 512 neighbouring positions
- cotangent: float32 [32, 1024, 768], P('dp', 'ctx'), may hold values from -6 to 6
- w_query: bfloat16 [768, 768], P(('dp', 'ctx')), may hold values from -0.21875 to 0.21875
- w_key: bfloat16 [768, 768], P(('dp', 'ctx')), may hold values from -0.21875 to 0.21875
- w_value: bfloat16 [768, 768], P(('dp', 'ctx')), may hold values from -0.21875 to 0.21875
- w_output: bfloat16 [768, 768], P(('dp', 'ctx')), may hold values from -1.75 to 1.75
- w_inner: bfloat16 [768, 3072], P(('dp', 'ctx')), may hold values from -0.21875 to 0.21875
- w_outer: bfloat16 [3072, 768], P(('dp', 'ctx')), may hold values from -0.109375 to 0.109375
- b_query: bfloat16 [768], P(('dp', 'ctx')), may hold values from -3 to 3
- b_value: bfloat16 [768], P(('dp', 'ctx')), may hold values from -3 to 3
- b_output: bfloat16 [768], P(('dp', 'ctx')), may hold values from -3 to 3
- gain_one: bfloat16 [768], P(('dp', 'ctx')), may hold values from 0.5 to 1.5
- shift_one: bfloat16 [768], P(('dp', 'ctx')), may hold values from -3 to 3
- b_inner: bfloat16 [3072], P(('dp', 'ctx')), may hold values from -3 to 3
- b_outer: bfloat16 [768], P(('dp', 'ctx')), may hold values from -3 to 3
- gain_two: bfloat16 [768], P(('dp', 'ctx')), may hold values from 0.5 to 1.5
- shift_two: bfloat16 [768], P(('dp', 'ctx')), may hold values from -3 to 3
Outputs:
- result: float32 [32, 1024, 768], P('dp', 'ctx')
- input_grad: float32 [32, 1024, 768], P('dp', 'ctx')
- grad_w_query: float32 [768, 768], P(('dp', 'ctx'))
- grad_w_key: float32 [768, 768], P(('dp', 'ctx'))
- grad_w_value: float32 [768, 768], P(('dp', 'ctx'))
- grad_w_output: float32 [768, 768], P(('dp', 'ctx'))
- grad_w_inner: float32 [768, 3072], P(('dp', 'ctx'))
- grad_w_outer: float32 [3072, 768], P(('dp', 'ctx'))
- grad_b_query: float32 [768], P(('dp', 'ctx'))
- grad_b_value: float32 [768], P(('dp', 'ctx'))
- grad_b_output: float32 [768], P(('dp', 'ctx'))
- grad_gain_one: float32 [768], P(('dp', 'ctx'))
- grad_shift_one: float32 [768], P(('dp', 'ctx'))
- grad_b_inner: float32 [3072], P(('dp', 'ctx'))
- grad_b_outer: float32 [768], P(('dp', 'ctx'))
- grad_gain_two: float32 [768], P(('dp', 'ctx'))
- grad_shift_two: float32 [768], P(('dp', 'ctx'))
Inputs may be any that keep to these rules, and one draw needn't show every extreme that they name: `segments`: within a sequence the document numbers never fall; a document has 1 to 512 tokens.
All inputs are finite; a program needn't handle non-finite values.
Results may differ from a plain program's by a relative error of at most 0.013.
The roundings to bfloat16 on the way count: a program that leaves them out, or rounds other values in their place, can miss the bound.
Values may be sent and summed in bfloat16 or wider, within the bound.
No kernel may reach another device: no remote copies, remote signals or barrier semaphores. Data moves between devices by JAX's collectives and lax.ppermute only.
A program may use at most 320 MiB of HBM per device.

v0:
```python
import jax
import jax.numpy as jnp
from jax import lax
from jax.sharding import PartitionSpec as P

HEADS = 12
HEAD_DIM = 64


EPSILON = 1e-12
MASKED_SCORE = -1e30


def as_sent(array):

    def short(part):
        return part.astype(jnp.bfloat16) if part.dtype == jnp.float32 else part

    return jax.tree.map(short, array)


def product(left_side, right_side):
    return jnp.dot(left_side, right_side, preferred_element_type=jnp.float32)


def times_transposed(left_side, right_side):
    return lax.dot_general(
        left_side, right_side, (((1,), (1,)), ((), ())), preferred_element_type=jnp.float32
    )


def transposed_times(left_side, right_side):
    return lax.dot_general(
        left_side, right_side, (((0,), (0,)), ((), ())), preferred_element_type=jnp.float32
    )


def layer_norm(summed, gain_vec, shift_vec):
    row_mean = jnp.mean(summed, -1, keepdims=True)
    centred = summed - row_mean
    variance = jnp.mean(centred * centred, -1, keepdims=True)
    inv_std = lax.rsqrt(variance + EPSILON)
    normed = centred * inv_std
    return (normed * gain_vec.astype(jnp.float32) + shift_vec.astype(jnp.float32), normed, inv_std)


def norm_back(upstream, normed, inv_std, gain_vec):
    scaled_grad = upstream * gain_vec.astype(jnp.float32)
    first_term = jnp.mean(scaled_grad, -1, keepdims=True)
    second_term = jnp.mean(scaled_grad * normed, -1, keepdims=True)
    return inv_std * (scaled_grad - first_term - normed * second_term)


def normal_parts(inner_pre):
    normal_cdf = 0.5 * (1.0 + lax.erf(inner_pre * 0.7071067811865476))
    normal_pdf = jnp.exp(-0.5 * inner_pre * inner_pre) * 0.3989422804014327
    return (normal_cdf, normal_pdf)


def masked_scores(queries, keys_all, same_doc):
    scores = jnp.einsum(
        "qhe,khe->hqk", queries, keys_all, preferred_element_type=jnp.float32
    ) * HEAD_DIM ** (-0.5)
    return jnp.where(same_doc[None], scores, MASKED_SCORE)


def attend(queries, keys_all, values_all, same_doc):
    scores = masked_scores(queries, keys_all, same_doc)
    top_score = jnp.max(scores, -1, keepdims=True)
    denominator = jnp.sum(jnp.exp(scores - top_score), -1, keepdims=True)
    log_total = top_score + jnp.log(denominator)
    probs_low = jnp.exp(scores - log_total).astype(jnp.bfloat16)
    context = jnp.einsum("hqk,khe->qhe", probs_low, values_all, preferred_element_type=jnp.float32)
    return (context, log_total)


def score_grads(queries, keys_all, values_all, same_doc, total_rows, grad_context_low, delta_rows):
    scores = masked_scores(queries, keys_all, same_doc)
    probs = jnp.exp(scores - jnp.transpose(total_rows)[:, :, None])
    probs_low = probs.astype(jnp.bfloat16)
    grad_probs = jnp.einsum(
        "qhe,khe->hqk", grad_context_low, values_all, preferred_element_type=jnp.float32
    )
    grad_scores = (
        probs * (grad_probs - jnp.transpose(delta_rows)[:, :, None]) * HEAD_DIM ** (-0.5)
    ).astype(jnp.bfloat16)
    return (probs_low, grad_scores)


def attend_back(queries, keys_all, values_all, same_doc, total_rows, grad_context_low, delta_rows):
    probs_low, grad_scores = score_grads(
        queries, keys_all, values_all, same_doc, total_rows, grad_context_low, delta_rows
    )
    grad_queries = jnp.einsum(
        "hqk,khe->qhe", grad_scores, keys_all, preferred_element_type=jnp.float32
    )
    grad_keys = jnp.einsum("hqk,qhe->khe", grad_scores, queries, preferred_element_type=jnp.float32)
    grad_values = jnp.einsum(
        "hqk,qhe->khe", probs_low, grad_context_low, preferred_element_type=jnp.float32
    )
    return (grad_queries, grad_keys, grad_values)


def matrix_grads(saved_rows):
    (
        inputs,
        grad_query_low,
        grad_key_low,
        grad_value_low,
        context_low,
        grad_first_low,
        first_low,
        grad_inner_low,
        activated,
        grad_second_low,
    ) = saved_rows
    return (
        transposed_times(inputs, grad_query_low),
        transposed_times(inputs, grad_key_low),
        transposed_times(inputs, grad_value_low),
        transposed_times(context_low, grad_first_low),
        transposed_times(first_low, grad_inner_low),
        transposed_times(activated, grad_second_low),
    )


def flat_shard(shard):
    return shard.reshape(1, -1)


def gathered_full(flat_whole, shard):
    return flat_whole.reshape((-1,) + shard.shape[1:])


def spread_rows(term, owners):
    return term.reshape(owners, -1)


def owned_rows(flat_owned, term):
    return flat_owned.reshape((-1,) + term.shape[1:])


def gather_params(shards, which):
    flats = tuple((flat_shard(shard) for shard in shards))
    if which == 0:
        wholes = jax.tree.map(
            lambda part, own: part.astype(own.dtype),
            lax.all_gather(as_sent(flats), ("dp", "ctx"), axis=0, tiled=True),
            flats,
        )
    else:
        wholes = jax.tree.map(
            lambda part, own: part.astype(own.dtype),
            lax.all_gather(as_sent(flats), ("dp", "ctx"), axis=0, tiled=True),
            flats,
        )
    return tuple((gathered_full(whole, shard) for whole, shard in zip(wholes, shards)))


def body(
    tokens,
    segments,
    cotangent,
    w_query,
    w_key,
    w_value,
    w_output,
    w_inner,
    w_outer,
    b_query,
    b_value,
    b_output,
    gain_one,
    shift_one,
    b_inner,
    b_outer,
    gain_two,
    shift_two,
):
    shards = (
        w_query,
        w_key,
        w_value,
        w_output,
        w_inner,
        w_outer,
        b_query,
        b_value,
        b_output,
        gain_one,
        shift_one,
        b_inner,
        b_outer,
        gain_two,
        shift_two,
    )
    owners = lax.axis_size(("dp", "ctx"))
    micro_count = tokens.shape[0]
    local_len = tokens.shape[1]
    model_width = tokens.shape[2]
    ctx_rank = lax.axis_index("ctx")
    result_list = []
    input_list = []
    saved_list = []
    vector_list = []
    owned_grads = None
    for micro_batch in range(micro_count):
        gathered = gather_params(shards, 0)
        query_mat, key_mat, value_mat, output_mat, inner_mat, outer_mat = gathered[:6]
        (
            query_bias,
            value_bias,
            output_bias,
            gain_first,
            shift_first,
            inner_bias,
            outer_bias,
            gain_second,
            shift_second,
        ) = gathered[6:]
        inputs = tokens[micro_batch]
        doc_ids = segments[micro_batch]
        own_ids = lax.dynamic_slice_in_dim(doc_ids, ctx_rank * local_len, local_len)
        same_doc = own_ids[:, None] == doc_ids[None, :]
        queries = (product(inputs, query_mat) + query_bias.astype(jnp.float32)).astype(jnp.bfloat16)
        keys_own = product(inputs, key_mat).astype(jnp.bfloat16)
        values_own = (product(inputs, value_mat) + value_bias.astype(jnp.float32)).astype(
            jnp.bfloat16
        )
        keys_all, values_all = (
            lax.all_gather(keys_own, "ctx", axis=0, tiled=True),
            lax.all_gather(values_own, "ctx", axis=0, tiled=True),
        )
        head_q = queries.reshape(local_len, HEADS, HEAD_DIM)
        head_k = keys_all.reshape(-1, HEADS, HEAD_DIM)
        head_v = values_all.reshape(-1, HEADS, HEAD_DIM)
        context, log_total = attend(head_q, head_k, head_v, same_doc)
        context_low = context.reshape(local_len, model_width).astype(jnp.bfloat16)
        first_sum = (
            inputs.astype(jnp.float32)
            + product(context_low, output_mat)
            + output_bias.astype(jnp.float32)
        )
        first_out, first_normed, first_rstd = layer_norm(first_sum, gain_first, shift_first)
        first_low = first_out.astype(jnp.bfloat16)
        inner_pre = product(first_low, inner_mat) + inner_bias.astype(jnp.float32)
        normal_cdf, normal_pdf = normal_parts(inner_pre)
        activated = (inner_pre * normal_cdf).astype(jnp.bfloat16)
        second_sum = first_out + product(activated, outer_mat) + outer_bias.astype(jnp.float32)
        result, second_normed, second_rstd = layer_norm(second_sum, gain_second, shift_second)
        result_list.append(result)
        back_params = gather_params(shards, 1)
        query_back, key_back, value_back, output_back, inner_back, outer_back = back_params[:6]
        gain_first_back = back_params[9]
        gain_second_back = back_params[13]
        grad_result = cotangent[micro_batch]
        grad_gain_two = jnp.sum(grad_result * second_normed, 0)
        grad_shift_two = jnp.sum(grad_result, 0)
        grad_second = norm_back(grad_result, second_normed, second_rstd, gain_second_back)
        grad_second_low = grad_second.astype(jnp.bfloat16)
        grad_outer_bias = jnp.sum(grad_second, 0)
        grad_act = times_transposed(grad_second_low, outer_back)
        grad_inner = grad_act * (normal_cdf + inner_pre * normal_pdf)
        grad_inner_low = grad_inner.astype(jnp.bfloat16)
        grad_inner_bias = jnp.sum(grad_inner, 0)
        grad_first_out = grad_second + times_transposed(grad_inner_low, inner_back)
        grad_gain_one = jnp.sum(grad_first_out * first_normed, 0)
        grad_shift_one = jnp.sum(grad_first_out, 0)
        grad_first = norm_back(grad_first_out, first_normed, first_rstd, gain_first_back)
        grad_first_low = grad_first.astype(jnp.bfloat16)
        grad_output_bias = jnp.sum(grad_first, 0)
        grad_context_flat = times_transposed(grad_first_low, output_back).astype(jnp.bfloat16)
        grad_context_low = grad_context_flat.reshape(local_len, HEADS, HEAD_DIM)
        total_rows = jnp.transpose(log_total[:, :, 0])
        delta_rows = jnp.sum(grad_context_low.astype(jnp.float32) * context, -1)
        grad_queries, key_terms, value_terms = attend_back(
            head_q, head_k, head_v, same_doc, total_rows, grad_context_low, delta_rows
        )
        grad_keys, grad_values = (
            lax.psum_scatter(
                key_terms.reshape(-1, model_width).astype(jnp.bfloat16),
                "ctx",
                scatter_dimension=0,
                tiled=True,
            ).astype(jnp.float32),
            lax.psum_scatter(
                value_terms.reshape(-1, model_width).astype(jnp.bfloat16),
                "ctx",
                scatter_dimension=0,
                tiled=True,
            ).astype(jnp.float32),
        )
        grad_queries = grad_queries.reshape(local_len, model_width)
        grad_query_low = grad_queries.astype(jnp.bfloat16)
        grad_key_low = grad_keys.astype(jnp.bfloat16)
        grad_value_low = grad_values.astype(jnp.bfloat16)
        input_grad = (
            grad_first
            + times_transposed(grad_query_low, query_back)
            + times_transposed(grad_key_low, key_back)
            + times_transposed(grad_value_low, value_back)
        )
        input_list.append(input_grad)
        saved_rows = (
            inputs,
            grad_query_low,
            grad_key_low,
            grad_value_low,
            context_low,
            grad_first_low,
            first_low,
            grad_inner_low,
            activated,
            grad_second_low,
        )
        vector_grads = (
            jnp.sum(grad_queries, 0),
            jnp.sum(grad_values, 0),
            grad_output_bias,
            grad_gain_one,
            grad_shift_one,
            grad_inner_bias,
            grad_outer_bias,
            grad_gain_two,
            grad_shift_two,
        )
        saved_list.append(saved_rows)
        vector_list.append(vector_grads)
    joined_rows = tuple(
        (jnp.concatenate([saved[index] for saved in saved_list], 0) for index in range(10))
    )
    summed_vectors = tuple((sum((vectors[index] for vectors in vector_list)) for index in range(9)))
    all_terms = matrix_grads(joined_rows) + summed_vectors
    flat_owned = lax.psum_scatter(
        tuple((spread_rows(term, owners) for term in all_terms)),
        ("dp", "ctx"),
        scatter_dimension=0,
        tiled=True,
    )
    owned_grads = tuple((owned_rows(flat, term) for flat, term in zip(flat_owned, all_terms)))
    results = jnp.stack(result_list, 0)
    input_grads = jnp.stack(input_list, 0)
    return (
        results,
        input_grads,
        owned_grads[0],
        owned_grads[1],
        owned_grads[2],
        owned_grads[3],
        owned_grads[4],
        owned_grads[5],
        owned_grads[6],
        owned_grads[7],
        owned_grads[8],
        owned_grads[9],
        owned_grads[10],
        owned_grads[11],
        owned_grads[12],
        owned_grads[13],
        owned_grads[14],
    )


def solution(mesh):
    in_specs = (
        P("dp", "ctx", None),
        P("dp", None),
        P("dp", "ctx", None),
        P(("dp", "ctx"), None),
        P(("dp", "ctx"), None),
        P(("dp", "ctx"), None),
        P(("dp", "ctx"), None),
        P(("dp", "ctx"), None),
        P(("dp", "ctx"), None),
        P(("dp", "ctx")),
        P(("dp", "ctx")),
        P(("dp", "ctx")),
        P(("dp", "ctx")),
        P(("dp", "ctx")),
        P(("dp", "ctx")),
        P(("dp", "ctx")),
        P(("dp", "ctx")),
        P(("dp", "ctx")),
    )
    out_specs = (
        P("dp", "ctx", None),
        P("dp", "ctx", None),
        P(("dp", "ctx"), None),
        P(("dp", "ctx"), None),
        P(("dp", "ctx"), None),
        P(("dp", "ctx"), None),
        P(("dp", "ctx"), None),
        P(("dp", "ctx"), None),
        P(("dp", "ctx")),
        P(("dp", "ctx")),
        P(("dp", "ctx")),
        P(("dp", "ctx")),
        P(("dp", "ctx")),
        P(("dp", "ctx")),
        P(("dp", "ctx")),
        P(("dp", "ctx")),
        P(("dp", "ctx")),
    )
    return jax.shard_map(body, mesh=mesh, in_specs=in_specs, out_specs=out_specs, check_vma=False)
```

profile of v0, /device:TPU:0, one launch (start us, length us, event | category | flops | bytes accessed | tf_op | source)
XLA Modules:
  0.0 1234.1 jit_solution(15741146917915283612)
XLA Ops:
  13.2 58.1 %all-gather.38.cloned.1.call-done = bf16[32,1,18432]{2,1,0:T(2,128)(2,1)} async-done(((bf16[1,1,18432]{2,1,0:T(2,128)(2,1)}), bf16[32,1,18432]{2,1,0:T(2,128)(2,1)}) %all-gather.38.cloned.1.call-update) | async-done | bytes 1179664 | tf_op jit(solution)/shard_map/all_gather | solution.py:148
  71.3 8.2 reduce.6
  81.4 3.0 convolution_convert_fusion.7
  86.7 39.4 %all-reduce.26 = (bf16[768]{0:T(1024)(128)(2,1)S(1)}, bf16[768]{0:T(1024)(128)(2,1)S(1)}, bf16[768]{0:T(1024)(128)(2,1)S(1)}, bf16[768]{0:T(1024)(128)(2,1)S(1)}...) all-reduce(bf16[768]{0:T(1024)(128)(2,1)S(1)} %dynamic-update-slice, ...), channel_id=2, replica_groups=mesh['dp'=16,'ctx'=2] {'dp','ctx'}, use_global_device_ids=true, to_apply=%add | all-reduce | flops 9216 | bytes 36864
  126.1 4.7 all-gather.34.cloned.1.call-done
  130.8 8.2 reduce.4
  139.6 3.3 add_convert_fusion.3
  144.8 3.0 convolution_convert_fusion.6
  152.4 37.9 %all-gather.36.cloned.1.call-done = bf16[32,1,18432]{2,1,0:T(2,128)(2,1)} async-done(((bf16[1,1,18432]{2,1,0:T(2,128)(2,1)}), bf16[32,1,18432]{2,1,0:T(2,128)(2,1)}) %all-gather.36.cloned.1.call-update) | async-done | bytes 1179664 | tf_op jit(solution)/shard_map/all_gather | solution.py:148
  190.4 8.2 reduce.5
  200.1 2.2 add_convert_fusion.2
  204.3 45.3 %all-gather.40.cloned.1.call-done = bf16[32,1,18432]{2,1,0:T(2,128)(2,1)} async-done(((bf16[1,1,18432]{2,1,0:T(2,128)(2,1)}), bf16[32,1,18432]{2,1,0:T(2,128)(2,1)}) %all-gather.40.cloned.1.call-update) | async-done | bytes 1179664 | tf_op jit(solution)/shard_map/all_gather | solution.py:148
  249.6 8.2 reduce.7
  260.7 17.0 %all-gather.28.cloned.1.call-done = bf16[1024,768]{1,0:T(8,128)(2,1)} async-done(((bf16[512,768]{1,0:T(8,128)(2,1)}), bf16[1024,768]{1,0:T(8,128)(2,1)}) %all-gather.28.cloned.1.call-update) | async-done | bytes 1572880 | tf_op jit(solution)/shard_map/all_gather | solution.py:231
  279.4 12.3 %fusion.2 = (f32[12,512]{1,0:T(8,128)S(1)}, f32[12,512,1024]{2,1,0:T(8,128)}) fusion(pred[512,1024]{1,0:T(8,128)(4,1)} %broadcast_compare_fusion.1, bf16[512,12,64]{0,2,1:T(8,128)(2,1)S(1)} %bitcast.178, bf16[1024,12,64]{0,2,1:T(8,128)(2,1)S(1)} %bitcast.174), kind=kOutput, calls=%fused_computation.10 | convolution fusion | flops 824174592 | bytes 28073984 | tf_op jit(solution)/shard_map/qhe,khe->hqk/dot_general | solution.py:61
  291.7 12.0 exponential_reduce_fusion.1
  303.7 3.1 all-gather.26.cloned.1.call-done
  306.8 2.6 copy.63
  309.4 26.2 %all-gather.30.cloned.1.call-done = bf16[1024,768]{1,0:T(8,128)(2,1)} async-done(((bf16[512,768]{1,0:T(8,128)(2,1)}), bf16[1024,768]{1,0:T(8,128)(2,1)}) %all-gather.30.cloned.1.call-update) | async-done | bytes 1572880 | tf_op jit(solution)/shard_map/all_gather | solution.py:232
  335.6 2.6 copy.66
  338.2 26.1 %all-gather.32.cloned.1.call-done = bf16[1024,768]{1,0:T(8,128)(2,1)} async-done(((bf16[512,768]{1,0:T(8,128)(2,1)}), bf16[1024,768]{1,0:T(8,128)(2,1)}) %all-gather.32.cloned.1.call-update) | async-done | bytes 1572880 | tf_op jit(solution)/shard_map/all_gather | solution.py:231
  366.1 13.1 %bitcast_convert_fusion.3 = (bf16[512,12,64]{0,2,1:T(8,128)(2,1)S(1)}, f32[12,64,512]{2,1,0:T(8,128)}) fusion(bf16[1024,12,64]{0,2,1:T(8,128)(2,1)} %bitcast.192, f32[12,512,1024]{2,1,0:T(8,128)} %get-tuple-element.88, f32[12,512]{1,0:T(8,128)S(1)} %log_add_fusion.1, pred[512,1024]{1,0:T(8,128)(4,1)S(1)} %copy-done.19), kind=kOutput, calls=%fused_computation.82 | convolution fusion | flops 830865408 | bytes 29646848 | tf_op jit(solution)/shard_map/hqk,khe->qhe/dot_general | solution.py:73
  381.6 10.5 fusion.3
  392.1 12.1 exponential_reduce_fusion
  404.2 12.5 %bitcast_convert_fusion.2 = (bf16[512,12,64]{0,2,1:T(8,128)(2,1)S(1)}, f32[12,64,512]{2,1,0:T(8,128)}) fusion(bf16[1024,12,64]{0,2,1:T(8,128)(2,1)S(1)} %bitcast.195, f32[12,512,1024]{2,1,0:T(8,128)} %get-tuple-element.94, f32[12,512]{1,0:T(8,128)S(1)} %log_add_fusion, pred[512,1024]{1,0:T(8,128)(4,1)S(1)} %copy-done.21), kind=kOutput, calls=%fused_computation.79 | convolution fusion | flops 830865408 | bytes 29646848 | tf_op jit(solution)/shard_map/hqk,khe->qhe/dot_general | solution.py:73
  419.8 29.6 %all-gather.42.cloned.1.call-done = bf16[32,1,73728]{2,1,0:T(2,128)(2,1)} async-done(((bf16[1,1,73728]{2,1,0:T(2,128)(2,1)}), bf16[32,1,73728]{2,1,0:T(2,128)(2,1)}) %all-gather.42.cloned.1.call-update) | async-done | bytes 4718608 | tf_op jit(solution)/shard_map/all_gather | solution.py:148
  449.4 29.2 %reduce.8 = bf16[32,73728]{1,0:T(8,128)(2,1)} reduce(bf16[32,1,73728]{2,1,0:T(2,128)(2,1)} %all-gather.42.cloned.1.call-done, bf16[]{:T(256)} %constant.147), dimensions={1}, to_apply=%all-gather.13.reduce_sub_computation | reduce | bytes 9437186 | tf_op jit(solution)/shard_map/all_gather | solution.py:148
  478.7 6.0 reshape.559
  484.7 48.1 %all-gather.44.cloned.1.call-done = bf16[32,1,73728]{2,1,0:T(2,128)(2,1)} async-done(((bf16[1,1,73728]{2,1,0:T(2,128)(2,1)}), bf16[32,1,73728]{2,1,0:T(2,128)(2,1)}) %all-gather.44.cloned.1.call-update) | async-done | bytes 4718608 | tf_op jit(solution)/shard_map/all_gather | solution.py:148
  532.8 29.2 %reduce.9 = bf16[32,73728]{1,0:T(8,128)(2,1)} reduce(bf16[32,1,73728]{2,1,0:T(2,128)(2,1)} %all-gather.44.cloned.1.call-done, bf16[]{:T(256)} %constant.147), dimensions={1}, to_apply=%all-gather.14.reduce_sub_computation | reduce | bytes 9437186 | tf_op jit(solution)/shard_map/all_gather | solution.py:148
  562.0 6.1 reshape.562
  568.1 4.8 fusion.95
  573.0 6.4 multiply_convert_fusion.3
  579.4 2.8 fusion.93
  582.6 2.8 fusion.94
  585.8 2.1 fusion.48
  587.9 3.1 fusion.85
  591.1 6.1 fusion.89
  597.2 5.0 multiply_reduce_fusion.1
  602.4 4.7 fusion.88
  607.1 4.9 fusion.87
  615.8 2.0 fusion.49
  617.8 17.5 %multiply_convert_fusion = bf16[12,512,1024]{2,1,0:T(8,128)(2,1)} fusion(f32[12,512,1024]{2,1,0:T(8,128)} %get-tuple-element.94, f32[12,512]{1,0:T(8,128)S(1)} %bitcast.202, f32[12,512]{1,0:T(8,128)S(1)} %log_add_fusion, pred[512,1024]{1,0:T(8,128)(4,1)S(1)} %copy-done.22, bf16[512,12,64]{0,2,1:T(8,128)(2,1)S(1)} %bitcast.187, bf16[1024,12,64]{0,2,1:T(8,128)(2,1)} %bitcast.194), kind=kOutput, calls=%fused_computation | convolution fusion | flops 849346560 | bytes 40681472 | tf_op jit(solution)/shard_map/qhe,khe->hqk/dot_general | solution.py:81
  635.3 8.1 convolution_convert_fusion.1
  650.3 17.8 %multiply_convert_fusion.1 = bf16[12,512,1024]{2,1,0:T(8,128)(2,1)} fusion(f32[12,512,1024]{2,1,0:T(8,128)} %get-tuple-element.88, f32[12,512]{1,0:T(8,128)S(1)} %bitcast.203, f32[12,512]{1,0:T(8,128)S(1)} %log_add_fusion.1, pred[512,1024]{1,0:T(8,128)(4,1)S(1)} %copy-done.20, bf16[512,12,64]{0,2,1:T(8,128)(2,1)S(1)} %bitcast.190, ...), kind=kOutput, calls=%fused_computation.1 | convolution fusion | flops 849346560 | bytes 40681472 | tf_op jit(solution)/shard_map/qhe,khe->hqk/dot_general | solution.py:81
  668.1 8.0 convolution_convert_fusion.3
  677.4 13.3 %convolution_convert_fusion = bf16[12,64,1024]{2,1,0:T(8,128)(2,1)} fusion(bf16[512,12,64]{0,2,1:T(8,128)(2,1)S(1)} %bitcast.188, f32[12,512,1024]{2,1,0:T(8,128)} %get-tuple-element.94, f32[12,512]{1,0:T(8,128)S(1)} %log_add_fusion, pred[512,1024]{1,0:T(8,128)(4,1)S(1)} %copy-done.23), kind=kOutput, calls=%fused_computation.38 | convolution fusion | flops 831258624 | bytes 28073984 | tf_op jit(solution)/shard_map/hqk,qhe->khe/dot_general | solution.py:98
  690.8 2.7 slice_bitcast_fusion.1
  693.5 10.0 bitcast_convert_fusion
  703.5 13.5 %convolution_convert_fusion.2 = bf16[12,64,1024]{2,1,0:T(8,128)(2,1)} fusion(bf16[512,12,64]{0,2,1:T(8,128)(2,1)S(1)} %bitcast.191, f32[12,512,1024]{2,1,0:T(8,128)} %get-tuple-element.88, f32[12,512]{1,0:T(8,128)S(1)} %log_add_fusion.1, pred[512,1024]{1,0:T(8,128)(4,1)S(1)} %copy-done.20), kind=kOutput, calls=%fused_computation.40 | convolution fusion | flops 831258624 | bytes 28073984 | tf_op jit(solution)/shard_map/hqk,qhe->khe/dot_general | solution.py:98
  718.4 9.8 bitcast_convert_fusion.1
  732.4 3.2 fusion.34
  737.3 9.9 fusion.14
  747.1 8.2 reshape.579
  755.4 9.5 fusion.18
  764.9 8.2 reshape.581
  773.1 3.0 fusion.26
  777.7 3.0 fusion.30
  786.6 2.1 bitcast_reduce_fusion
  795.4 46.0 %all-reduce.24 = (f32[32,24]{1,0:T(8,128)S(1)}, f32[32,24]{1,0:T(8,128)S(1)}, f32[32,24]{1,0:T(8,128)S(1)}, f32[32,24]{1,0:T(8,128)S(1)}, f32[32,24]{1,0:T(8,128...) all-reduce(f32[32,24]{1,0:T(8,128)S(1)} %add.344, ...), channel_id=21, replica_groups=mesh['dp'=16,'ctx'=2] {'dp','ctx'}, use_global_device_ids=true, to_apply=%region_34.35.clone | all-reduce | flops 9216 | bytes 73728
  846.1 2.5 fusion.99
  854.8 358.3 %all-reduce.29.cloned.1.call-done = (f32[32,18432]{1,0:T(8,128)}, f32[32,18432]{1,0:T(8,128)}, f32[32,18432]{1,0:T(8,128)}, f32[32,18432]{1,0:T(8,128)}, f32[32,73728]{1,0:T(8,128)}, /*index=5*/f32[32,73728]{1,0:T(8,128)}) async-done(((f32[32,18432]{1,0:T(8,128)}, f32[32,18432]{1,0:T(8,128)}, f32[32,18432]{1,0:T(8,128)}, f32[32,18432]{1,0:T(8,128)}, f32[32,73728]{1,0:T(8,128)}, ...) | async-done | bytes 28311568
  1220.7 2.4 dynamic-slice_reduce_fusion.1
  1223.9 2.4 dynamic-slice_reduce_fusion
  (335 shorter events, 86.0 us)
Async XLA Ops:
  7.2 64.1 %all-gather.38.cloned.1.call-start = ((), (), s32[]{:S(2)}) async-start(), calls=%async_computation.14 | async-start | bytes 2433024 | tf_op jit(solution)/shard_map/all_gather | solution.py:148
  8.7 122.1 %all-gather.34.cloned.1.call-start = ((), (), s32[]{:S(2)}) async-start(), calls=%async_computation.12 | async-start | bytes 2433024 | tf_op jit(solution)/shard_map/all_gather | solution.py:148
  10.2 180.2 %all-gather.36.cloned.1.call-start = ((), (), s32[]{:S(2)}) async-start(), calls=%async_computation.13 | async-start | bytes 2433024 | tf_op jit(solution)/shard_map/all_gather | solution.py:148
  11.7 238.0 %all-gather.40.cloned.1.call-start = ((), (), s32[]{:S(2)}) async-start(), calls=%async_computation.15 | async-start | bytes 2433024 | tf_op jit(solution)/shard_map/all_gather | solution.py:148
  13.2 264.5 %all-gather.28.cloned.1.call-start = ((), (), s32[]{:S(2)}) async-start(), calls=%async_computation.5 | async-start | bytes 2359296 | tf_op jit(solution)/shard_map/all_gather | solution.py:231
  81.4 3.2 copy-start.64
  81.4 3.4 copy-start.65
  81.4 3.7 copy-start.66
  81.4 3.9 copy-start.67
  81.4 4.1 copy-start.68
  81.4 4.4 copy-start.69
  81.4 4.6 copy-start.70
  81.4 4.8 copy-start.71
  81.4 5.0 copy-start.72
  84.5 222.3 %all-gather.26.cloned.1.call-start = ((), (), s32[]{:S(2)}) async-start(), calls=%async_computation.4 | async-start | bytes 2359296 | tf_op jit(solution)/shard_map/all_gather | solution.py:232
  139.6 3.4 copy-start.8
  139.6 3.4 copy-start.30
  142.9 192.7 %all-gather.30.cloned.1.call-start = ((), (), s32[]{:S(2)}) async-start(), calls=%async_computation.6 | async-start | bytes 2359296 | tf_op jit(solution)/shard_map/all_gather | solution.py:232
  144.7 3.1 copy-start.55
  144.7 219.6 %all-gather.32.cloned.1.call-start = ((), (), s32[]{:S(2)}) async-start(), calls=%async_computation.7 | async-start | bytes 2359296 | tf_op jit(solution)/shard_map/all_gather | solution.py:231
  147.8 301.7 %all-gather.42.cloned.1.call-start = ((), (), s32[]{:S(2)}) async-start(), calls=%async_computation.16 | async-start | bytes 9732096 | tf_op jit(solution)/shard_map/all_gather | solution.py:148
  148.7 384.1 %all-gather.44.cloned.1.call-start = ((), (), s32[]{:S(2)}) async-start(), calls=%async_computation.17 | async-start | bytes 9732096 | tf_op jit(solution)/shard_map/all_gather | solution.py:148
  149.5 623.5 %reduce-scatter.9.cloned.1.call-start = ((), (), s32[]{:S(2)}) async-start(), calls=%async_computation.10 | async-start | bytes 2359296 | tf_op jit(solution)/shard_map/reduce_scatter | solution.py:280
  204.3 75.0 %copy-start.10 = (bf16[512,768]{0,1:T(8,128)(2,1)}, bf16[512,768]{0,1:T(8,128)(2,1)S(1)}, u32[]{:S(2)}) copy-start(bf16[512,768]{0,1:T(8,128)(2,1)S(1)} %copy.64) | copy-start | bytes 2359300
  279.3 12.4 %copy-start.4 = (bf16[1024,768]{0,1:T(8,128)(2,1)}, bf16[1024,768]{0,1:T(8,128)(2,1)S(1)}, u32[]{:S(2)}) copy-start(bf16[1024,768]{0,1:T(8,128)(2,1)S(1)} %copy.65) | copy-start | bytes 4718596
  279.4 12.4 %copy-start.18 = (pred[512,1024]{1,0:T(8,128)(4,1)S(1)}, pred[512,1024]{1,0:T(8,128)(4,1)}, u32[]{:S(2)}) copy-start(pred[512,1024]{1,0:T(8,128)(4,1)} %broadcast_compare_fusion.1) | copy-start | bytes 1572868
  338.2 27.9 %copy-start.19 = (pred[512,1024]{1,0:T(8,128)(4,1)S(1)}, pred[512,1024]{1,0:T(8,128)(4,1)}, u32[]{:S(2)}) copy-start(pred[512,1024]{1,0:T(8,128)(4,1)} %broadcast_compare_fusion.1) | copy-start | bytes 1572868
  366.1 14.4 %copy-start.6 = (bf16[1024,768]{0,1:T(8,128)(2,1)}, bf16[1024,768]{0,1:T(8,128)(2,1)S(1)}, u32[]{:S(2)}) copy-start(bf16[1024,768]{0,1:T(8,128)(2,1)S(1)} %copy.68) | copy-start | bytes 4718596
  366.1 13.1 %copy-start.31 = (bf16[2,512,768]{2,1,0:T(8,128)(2,1)S(1)}, bf16[2,512,768]{2,1,0:T(8,128)(2,1)}, u32[]{:S(2)}) copy-start(bf16[2,512,768]{2,1,0:T(8,128)(2,1)} %param.18) | copy-start | bytes 4718596
  366.1 13.1 %copy-start.38 = (bf16[768,768]{1,0:T(8,128)(2,1)S(1)}, bf16[768,768]{1,0:T(8,128)(2,1)}, u32[]{:S(2)}) copy-start(bf16[768,768]{1,0:T(8,128)(2,1)} %reshape.554) | copy-start | bytes 3538948
  380.2 37.9 %copy-start.14 = (f32[512,768]{1,0:T(8,128)}, f32[512,768]{1,0:T(8,128)S(1)}, u32[]{:S(2)}) copy-start(f32[512,768]{1,0:T(8,128)S(1)} %get-tuple-element.92) | copy-start | bytes 4718596
  392.1 12.1 copy-start.33
  562.0 11.0 slice-start
  568.1 4.8 slice-start.1
  568.1 4.8 copy-start.45
  568.1 11.3 slice-start.2
  573.0 6.5 copy-start.15
  573.0 6.4 slice-start.3
  579.4 2.9 copy-start.75
  579.4 3.2 copy-start.76
  582.6 3.1 copy-start
  591.1 6.1 copy-start.46
  602.4 4.7 copy-start.48
  607.1 4.9 copy-start.77
  615.7 19.5 %copy-start.25 = (bf16[512,768]{0,1:T(8,128)(2,1)}, bf16[512,768]{0,1:T(8,128)(2,1)S(1)}, u32[]{:S(2)}) copy-start(bf16[512,768]{0,1:T(8,128)(2,1)S(1)} %copy.70) | copy-start | bytes 2359300
  643.4 129.6 %reduce-scatter.5.cloned.1.call-start = ((), (), s32[]{:S(2)}) async-start(), calls=%async_computation.8 | async-start | bytes 2359296 | tf_op jit(solution)/shard_map/reduce_scatter | solution.py:280
  650.3 17.8 %copy-start.11 = (bf16[512,768]{0,1:T(8,128)(2,1)S(1)}, bf16[512,768]{0,1:T(8,128)(2,1)}, u32[]{:S(2)}) copy-start(bf16[512,768]{0,1:T(8,128)(2,1)} %copy-done.10) | copy-start | bytes 2359300
  676.2 101.6 %reduce-scatter.11.cloned.1.call-start = ((), (), s32[]{:S(2)}) async-start(), calls=%async_computation.11 | async-start | bytes 2359296 | tf_op jit(solution)/shard_map/reduce_scatter | solution.py:286
  690.8 87.0 %reduce-scatter.7.cloned.1.call-start = ((), (), s32[]{:S(2)}) async-start(), calls=%async_computation.9 | async-start | bytes 2359296 | tf_op jit(solution)/shard_map/reduce_scatter | solution.py:286
  717.0 12.1 copy-start.41
  717.0 496.0 %all-reduce.29.cloned.1.call-start = ((), (), s32[]{:S(2)}) async-start(), calls=%async_computation.18 | async-start | bytes 56623104
  718.4 10.7 copy-start.52
  718.4 10.7 copy-start.54
  747.1 8.3 copy-start.47
  747.1 8.3 copy-start.49
  764.9 8.2 copy-start.53
  784.8 4.3 copy-start.61
  784.8 4.3 copy-start.57
  784.8 4.3 copy-start.58
  784.8 4.4 copy-start.59
  784.8 4.4 copy-start.60
  784.8 4.5 copy-start.12
  784.8 4.5 copy-start.13
  846.1 3.4 copy-start.34
  (33 other events, 54.3 us)
Sparse Core Ops, SparseCore 0:
  11.5 59.8 all-gather.37
  74.8 55.9 all-gather.33
  134.3 55.9 all-gather.35
  193.7 55.8 all-gather.39
  251.6 25.9 all-gather.27
  279.6 27.1 all-gather.25
  308.4 27.1 all-gather.29
  337.1 27.1 all-gather.31
  367.8 81.5 all-gather.41
  452.8 79.9 all-gather.43
  643.5 24.6 reduce-scatter.8
  676.3 24.7 reduce-scatter.4
  703.3 26.1 reduce-scatter.10
  731.6 26.1 reduce-scatter.6
  782.7 430.2 all-reduce.28
where the time goes:
time: 1240 us; the launch traced here: 1230 us
  waiting for transfers between devices  655 us (53%)
  matrix products  241 us (19%)
  other arithmetic  137 us (11%)
  local copies, waits for them, and re-layouts  99.1 us (8%)
  blocking collectives  85.4 us (7%)
  between operations  15.7 us (1%)
    unnamed x16, waiting for transfers between devices  359 us
    all_gather x6, waiting for transfers between devices, gather_params(): lax.all_gather(as_sent(flats), ('dp', 'ctx'), axis=0, tiled=True)  224 us
    all_gather x6, other arithmetic, gather_params(): lax.all_gather(as_sent(flats), ('dp', 'ctx'), axis=0, tiled=True)  91.2 us
    unnamed x2, blocking collectives  85.4 us
    all_gather x2, waiting for transfers between devices, body(): lax.all_gather(keys_own, 'ctx', axis=0, tiled=True)  43.1 us
    dot_general x2, matrix products, score_grads(): jnp.einsum('qhe,khe->hqk', grad_context_low, values_all, preferred_elemen...  35.4 us
    unnamed x194, local copies, waits for them, and re-layouts  34 us
    dot_general x12, matrix products, product(): return jnp.dot(left_side, right_side, preferred_element_type=jnp.float32)  33.5 us
  transfers between devices with their start and end apart: 15, of which 11 were waited for; matrix products, arithmetic and copies ran while one was open for 27% of the time, Pallas kernels for 0%

commit v1 on v0

v1 whole, which is shorter than its diff:
```python
import functools

import jax
import jax.numpy as jnp
from jax import lax
from jax.experimental import pallas as pl
from jax.experimental.pallas import tpu as pltpu
from jax.sharding import PartitionSpec as P

HEAD_DIM = 64
EPSILON = 1e-12
MASKED_SCORE = -1e30
LANES = 128
HEAD_PAIR = LANES // HEAD_DIM
SCALE = HEAD_DIM**-0.5
KEY_STEP = 256

WIDE = jnp.float32
LOW = jnp.bfloat16


def product(left_side, right_side):
    return jnp.dot(left_side, right_side, preferred_element_type=WIDE)


def times_transposed(left_side, right_side):
    return lax.dot_general(
        left_side, right_side, (((1,), (1,)), ((), ())), preferred_element_type=WIDE
    )


def transposed_times(left_side, right_side):
    return lax.dot_general(
        left_side, right_side, (((0,), (0,)), ((), ())), preferred_element_type=WIDE
    )


def layer_norm(summed, gain_vec, shift_vec):
    row_mean = jnp.mean(summed, -1, keepdims=True)
    centred = summed - row_mean
    variance = jnp.mean(centred * centred, -1, keepdims=True)
    inv_std = lax.rsqrt(variance + EPSILON)
    normed = centred * inv_std
    return (normed * gain_vec + shift_vec, normed, inv_std)


def norm_back(upstream, normed, inv_std, gain_vec):
    scaled_grad = upstream * gain_vec
    first_term = jnp.mean(scaled_grad, -1, keepdims=True)
    second_term = jnp.mean(scaled_grad * normed, -1, keepdims=True)
    return inv_std * (scaled_grad - first_term - normed * second_term)


def normal_parts(inner_pre):
    normal_cdf = 0.5 * (1.0 + lax.erf(inner_pre * 0.7071067811865476))
    normal_pdf = jnp.exp(-0.5 * inner_pre * inner_pre) * 0.3989422804014327
    return (normal_cdf, normal_pdf)


def key_ranges(own_ids, doc_ids, block):
    total = doc_ids.shape[-1]
    blocks = own_ids.reshape(own_ids.shape[0], -1, block)
    first = blocks[:, :, 0]
    last = blocks[:, :, -1]
    begin = jnp.sum(doc_ids[:, None, :] < first[:, :, None], -1, dtype=jnp.int32)
    end = jnp.sum(doc_ids[:, None, :] <= last[:, :, None], -1, dtype=jnp.int32)
    start = begin // LANES
    steps = (end - start * LANES + KEY_STEP - 1) // KEY_STEP
    start = jnp.minimum(start, (total - steps * KEY_STEP) // LANES)
    return jnp.stack([start, steps - 1], -1).reshape(-1)


def head_lanes(rows, head):
    lane = lax.broadcasted_iota(jnp.int32, (rows, LANES), 1)
    return (lane >= head * HEAD_DIM) & (lane < (head + 1) * HEAD_DIM)


def only_head(array, head):
    return jnp.where(head_lanes(array.shape[0], head), array, jnp.zeros_like(array))


def by_width(steps, most, branch):
    lax.switch(steps, [functools.partial(branch, (n + 1) * KEY_STEP) for n in range(most)])


def masked(scores_t, key_ids, query_ids):
    wide_ids = jnp.tile(key_ids, (1, scores_t.shape[1] // LANES))
    return jnp.where(wide_ids == query_ids, scores_t, MASKED_SCORE)


def attend_kernel(block, ranges, q_ref, k_ref, v_ref, qid_ref, kid_ref, ctx_ref, low_ref, lse_ref):
    count = q_ref.shape[1] // block
    total = k_ref.shape[1]
    base = pl.program_id(0) * count

    def one_block(index, carry):
        rows = pl.ds(pl.multiple_of(index * block, block), block)
        start = pl.multiple_of(ranges[2 * (base + index)] * LANES, LANES)
        steps = ranges[2 * (base + index) + 1]

        def branch(width):
            keys = pl.ds(start, width)
            key_part = k_ref[0, keys, :]
            value_part = v_ref[0, keys, :]
            key_ids = kid_ref[0, keys, :]
            query_ids = qid_ref[0, :, rows]
            query_part = q_ref[0, rows, :] * jnp.asarray(SCALE, LOW)
            parts = []
            for head in range(HEAD_PAIR):
                scores = times_transposed(key_part, only_head(query_part, head))
                scores = masked(scores, key_ids, query_ids)
                top = jnp.max(scores, 0, keepdims=True)
                powers = jnp.exp(scores - top)
                denominator = jnp.sum(powers, 0, keepdims=True)
                probs_low = (powers * (1.0 / denominator)).astype(LOW)
                lse_ref[0, 0, head : head + 1, rows] = top + jnp.log(denominator)
                both = transposed_times(value_part, probs_low)
                parts.append(both[head * HEAD_DIM : (head + 1) * HEAD_DIM])
            context = jnp.transpose(jnp.concatenate(parts, 0))
            ctx_ref[0, rows, :] = context
            low_ref[0, rows, :] = context.astype(LOW)

        by_width(steps, total // KEY_STEP, branch)
        return carry

    lax.fori_loop(0, count, one_block, 0)


def attend_back_kernel(
    block,
    ranges,
    q_ref,
    k_ref,
    v_ref,
    g_ref,
    ctx_ref,
    lse_ref,
    qid_ref,
    kid_ref,
    dq_ref,
    dk_ref,
    dv_ref,
    dk_sum,
    dv_sum,
):
    count = q_ref.shape[1] // block
    total = k_ref.shape[1]
    base = pl.program_id(0) * count
    dk_sum[...] = jnp.zeros_like(dk_sum)
    dv_sum[...] = jnp.zeros_like(dv_sum)

    def one_block(index, carry):
        rows = pl.ds(pl.multiple_of(index * block, block), block)
        start = pl.multiple_of(ranges[2 * (base + index)] * LANES, LANES)
        steps = ranges[2 * (base + index) + 1]

        def branch(width):
            keys = pl.ds(start, width)
            key_part = k_ref[0, keys, :]
            value_part = v_ref[0, keys, :] * jnp.asarray(SCALE, LOW)
            key_ids = kid_ref[0, keys, :]
            query_ids = qid_ref[0, :, rows]
            query_part = q_ref[0, rows, :]
            grad_part = g_ref[0, rows, :]
            products = jnp.transpose(grad_part.astype(WIDE) * ctx_ref[0, rows, :])
            dq_parts = []
            dk_total = None
            dv_total = None
            for head in range(HEAD_PAIR):
                query_head = only_head(query_part, head)
                grad_head = only_head(grad_part, head)
                scores = times_transposed(key_part, query_head * jnp.asarray(SCALE, LOW))
                scores = masked(scores, key_ids, query_ids)
                probs = jnp.exp(scores - lse_ref[0, 0, head : head + 1, rows])
                probs_low = probs.astype(LOW)
                delta = SCALE * jnp.sum(
                    products[head * HEAD_DIM : (head + 1) * HEAD_DIM], 0, keepdims=True
                )
                grad_probs = times_transposed(value_part, grad_head)
                grad_scores = (probs * (grad_probs - delta)).astype(LOW)
                dv_part = product(probs_low, grad_head)
                dk_part = product(grad_scores, query_head)
                dq_parts.append(transposed_times(grad_scores, key_part))
                dk_total = dk_part if dk_total is None else dk_total + dk_part
                dv_total = dv_part if dv_total is None else dv_total + dv_part
            dq = dq_parts[0]
            for head in range(1, HEAD_PAIR):
                dq = jnp.where(head_lanes(block, head), dq_parts[head], dq)
            dq_ref[0, rows, :] = dq.astype(LOW)
            dk_sum[keys, :] += dk_total
            dv_sum[keys, :] += dv_total

        by_width(steps, total // KEY_STEP, branch)
        return carry

    lax.fori_loop(0, count, one_block, 0)
    dk_ref[0] = dk_sum[...].astype(LOW)
    dv_ref[0] = dv_sum[...].astype(LOW)


def attention_specs(queries, keys_all, block):
    seqs, length, width = queries.shape
    total = keys_all.shape[1]
    pairs = width // LANES
    per_query = pl.BlockSpec((1, length, LANES), lambda s, h, _: (s, 0, h))
    per_key = pl.BlockSpec((1, total, LANES), lambda s, h, _: (s, 0, h))
    lse_spec = pl.BlockSpec((1, 1, HEAD_PAIR, length), lambda s, h, _: (s, h, 0, 0))
    qid_spec = pl.BlockSpec((1, 1, length), lambda s, h, _: (s, 0, 0))
    kid_spec = pl.BlockSpec((1, total, LANES), lambda s, h, _: (s, 0, 0))
    return (seqs, pairs), per_query, per_key, lse_spec, qid_spec, kid_spec


def attend(queries, keys_all, values_all, tables):
    ranges, query_ids, key_ids, block = tables
    grid, per_query, per_key, lse_spec, qid_spec, kid_spec = attention_specs(
        queries, keys_all, block
    )
    seqs, length, width = queries.shape
    return pl.pallas_call(
        functools.partial(attend_kernel, block),
        grid_spec=pltpu.PrefetchScalarGridSpec(
            num_scalar_prefetch=1,
            grid=grid,
            in_specs=[per_query, per_key, per_key, qid_spec, kid_spec],
            out_specs=[per_query, per_query, lse_spec],
        ),
        out_shape=[
            jax.ShapeDtypeStruct(queries.shape, WIDE),
            jax.ShapeDtypeStruct(queries.shape, LOW),
            jax.ShapeDtypeStruct((seqs, grid[1], HEAD_PAIR, length), WIDE),
        ],
        name="attend",
    )(ranges, queries, keys_all, values_all, query_ids, key_ids)


def attend_back(queries, keys_all, values_all, grad_context, context, lse, tables):
    ranges, query_ids, key_ids, block = tables
    grid, per_query, per_key, lse_spec, qid_spec, kid_spec = attention_specs(
        queries, keys_all, block
    )
    total = keys_all.shape[1]
    return pl.pallas_call(
        functools.partial(attend_back_kernel, block),
        grid_spec=pltpu.PrefetchScalarGridSpec(
            num_scalar_prefetch=1,
            grid=grid,
            in_specs=[
                per_query,
                per_key,
                per_key,
                per_query,
                per_query,
                lse_spec,
                qid_spec,
                kid_spec,
            ],
            out_specs=[per_query, per_key, per_key],
            scratch_shapes=[pltpu.VMEM((total, LANES), WIDE), pltpu.VMEM((total, LANES), WIDE)],
        ),
        out_shape=[
            jax.ShapeDtypeStruct(queries.shape, LOW),
            jax.ShapeDtypeStruct(keys_all.shape, LOW),
            jax.ShapeDtypeStruct(keys_all.shape, LOW),
        ],
        name="attend_back",
    )(ranges, queries, keys_all, values_all, grad_context, context, lse, query_ids, key_ids)


def swap_in(array, ranks, rank):
    part = array.shape[1]
    whole = jnp.zeros((1, ranks * part) + array.shape[2:], array.dtype)
    for shift in range(ranks):
        other = (rank + shift) % ranks
        piece = lax.dynamic_slice_in_dim(array, other, 1, 0)
        if shift:
            piece = lax.ppermute(piece, "ctx", [(i, (i + shift) % ranks) for i in range(ranks)])
        source = (rank + ranks - shift) % ranks
        whole = lax.dynamic_update_slice_in_dim(whole, piece, source * part, 1)
    return whole


def swap_out(array, ranks, rank):
    part = array.shape[1] // ranks
    spread = jnp.zeros((ranks, part) + array.shape[2:], array.dtype)
    for shift in range(ranks):
        other = (rank + shift) % ranks
        piece = lax.dynamic_slice_in_dim(array, other * part, part, 1)
        if shift:
            piece = lax.ppermute(piece, "ctx", [(i, (i + shift) % ranks) for i in range(ranks)])
        source = (rank + ranks - shift) % ranks
        spread = lax.dynamic_update_slice_in_dim(spread, piece, source, 0)
    return spread


def pack_blocks(matrices, vectors, width, lead):
    blocks = []
    for matrix in matrices:
        rows, columns = matrix.shape[-2:]
        if columns == width:
            blocks.append(matrix)
        else:
            for at in range(columns // width):
                blocks.append(matrix[..., at * width : (at + 1) * width])
    line = jnp.concatenate(vectors, -1)
    size = line.shape[-1]
    lines = -(-size // width)
    lines = -(-lines // 8) * 8
    pad = [(0, 0)] * lead + [(0, lines * width - size)]
    blocks.append(jnp.pad(line, pad).reshape(line.shape[:-1] + (lines, width)))
    return jnp.concatenate(blocks, -2)


def unpack_blocks(packed, matrices, vectors, width):
    out = []
    at = 0
    for matrix in matrices:
        rows, columns = matrix.shape
        pieces = []
        for _ in range(columns // width):
            pieces.append(packed[..., at : at + rows, :])
            at += rows
        out.append(pieces[0] if len(pieces) == 1 else jnp.concatenate(pieces, -1))
    line = packed[..., at:, :].reshape(packed.shape[:-2] + (-1,))
    at = 0
    for vector in vectors:
        size = vector.shape[0]
        out.append(line[..., at : at + size])
        at += size
    return out


def body(tokens, segments, cotangent, *shards):
    matrices, vectors = shards[:6], shards[6:]
    owners = lax.axis_size(("dp", "ctx"))
    ranks = lax.axis_size("ctx")
    rank = lax.axis_index("ctx")
    micro_count, local_len, width = tokens.shape
    whole_here = micro_count == ranks

    with jax.named_scope("gather"):
        packed = pack_blocks(matrices, vectors, width, 0)
        gathered = lax.all_gather(packed, ("dp", "ctx"), axis=0, tiled=False)
        wholes = unpack_blocks(gathered, matrices, vectors, width)
        query_mat, key_mat, value_mat, output_mat, inner_mat, outer_mat = [
            whole.reshape((-1,) + whole.shape[2:]) for whole in wholes[:6]
        ]
        (
            query_bias,
            value_bias,
            output_bias,
            gain_first,
            shift_first,
            inner_bias,
            outer_bias,
            gain_second,
            shift_second,
        ) = [whole.reshape(-1).astype(WIDE) for whole in wholes[6:]]

    with jax.named_scope("swap_in"):
        if whole_here:
            inputs = swap_in(tokens, ranks, rank)
            grad_result = swap_in(cotangent, ranks, rank)
            doc_ids = lax.dynamic_slice_in_dim(segments, rank, 1, 0)
            own_ids = doc_ids
        else:
            inputs, grad_result, doc_ids = tokens, cotangent, segments
            own_ids = lax.dynamic_slice_in_dim(doc_ids, rank * local_len, local_len, 1)
    seqs, length, _ = inputs.shape
    total = doc_ids.shape[1]
    block = min(256, length)
    tables = (
        key_ranges(own_ids, doc_ids, block),
        own_ids[:, None, :],
        jnp.broadcast_to(doc_ids[:, :, None], doc_ids.shape + (LANES,)),
        block,
    )
    by_seq = lambda array: array.reshape(seqs, -1, width)
    inputs = inputs.reshape(-1, width)
    grad_result = grad_result.reshape(-1, width)

    def all_keys(own):
        own = by_seq(own)
        return own if whole_here else lax.all_gather(own, "ctx", axis=1, tiled=True)

    def own_keys(terms):
        if not whole_here:
            terms = lax.psum_scatter(terms, "ctx", scatter_dimension=1, tiled=True)
        return terms.reshape(-1, width)

    with jax.named_scope("forward"):
        queries = by_seq((product(inputs, query_mat) + query_bias).astype(LOW))
        keys_all = all_keys(product(inputs, key_mat).astype(LOW))
        values_all = all_keys((product(inputs, value_mat) + value_bias).astype(LOW))
        context, context_low, lse = attend(queries, keys_all, values_all, tables)
        context_low = context_low.reshape(-1, width)
        first_sum = inputs.astype(WIDE) + product(context_low, output_mat) + output_bias
        first_out, first_normed, first_rstd = layer_norm(first_sum, gain_first, shift_first)
        first_low = first_out.astype(LOW)
        inner_pre = product(first_low, inner_mat) + inner_bias
        normal_cdf, normal_pdf = normal_parts(inner_pre)
        activated = (inner_pre * normal_cdf).astype(LOW)
        second_sum = first_out + product(activated, outer_mat) + outer_bias
        result, second_normed, second_rstd = layer_norm(second_sum, gain_second, shift_second)

    with jax.named_scope("backward"):
        grad_gain_two = jnp.sum(grad_result * second_normed, 0)
        grad_shift_two = jnp.sum(grad_result, 0)
        grad_second = norm_back(grad_result, second_normed, second_rstd, gain_second)
        grad_second_low = grad_second.astype(LOW)
        grad_outer_bias = jnp.sum(grad_second, 0)
        grad_act = times_transposed(grad_second_low, outer_mat)
        grad_inner = grad_act * (normal_cdf + inner_pre * normal_pdf)
        grad_inner_low = grad_inner.astype(LOW)
        grad_inner_bias = jnp.sum(grad_inner, 0)
        grad_first_out = grad_second + times_transposed(grad_inner_low, inner_mat)
        grad_gain_one = jnp.sum(grad_first_out * first_normed, 0)
        grad_shift_one = jnp.sum(grad_first_out, 0)
        grad_first = norm_back(grad_first_out, first_normed, first_rstd, gain_first)
        grad_first_low = grad_first.astype(LOW)
        grad_output_bias = jnp.sum(grad_first, 0)
        grad_context = by_seq(times_transposed(grad_first_low, output_mat).astype(LOW))
        dq, dk, dv = attend_back(
            queries, keys_all, values_all, grad_context, context, lse, tables
        )
        grad_query_low = dq.reshape(-1, width)
        grad_key_low = own_keys(dk)
        grad_value_low = own_keys(dv)
        input_grad = (
            grad_first
            + times_transposed(grad_query_low, query_mat)
            + times_transposed(grad_key_low, key_mat)
            + times_transposed(grad_value_low, value_mat)
        )
        matrix_terms = (
            transposed_times(inputs, grad_query_low),
            transposed_times(inputs, grad_key_low),
            transposed_times(inputs, grad_value_low),
            transposed_times(context_low, grad_first_low),
            transposed_times(first_low, grad_inner_low),
            transposed_times(activated, grad_second_low),
        )
        vector_terms = (
            jnp.sum(grad_query_low.astype(WIDE), 0),
            jnp.sum(grad_value_low.astype(WIDE), 0),
            grad_output_bias,
            grad_gain_one,
            grad_shift_one,
            grad_inner_bias,
            grad_outer_bias,
            grad_gain_two,
            grad_shift_two,
        )

    with jax.named_scope("scatter"):
        packed_terms = pack_blocks(
            [term.astype(LOW).reshape(owners, -1, term.shape[1]) for term in matrix_terms],
            [term.astype(LOW).reshape(owners, -1) for term in vector_terms],
            width,
            1,
        )
        owned = lax.psum_scatter(
            packed_terms, ("dp", "ctx"), scatter_dimension=0, tiled=False
        ).astype(WIDE)
        owned_grads = unpack_blocks(owned, matrices, vectors, width)

    with jax.named_scope("swap_out"):
        if whole_here:
            results = swap_out(by_seq(result), ranks, rank)
            input_grads = swap_out(by_seq(input_grad).astype(LOW), ranks, rank).astype(WIDE)
        else:
            results, input_grads = by_seq(result), by_seq(input_grad)
    return (results, input_grads) + tuple(owned_grads)


def solution(mesh):
    by_tokens = P("dp", "ctx", None)
    matrix = P(("dp", "ctx"), None)
    vector = P(("dp", "ctx"))
    grads = (matrix,) * 6 + (vector,) * 9
    in_specs = (by_tokens, P("dp", None), by_tokens) + grads
    out_specs = (by_tokens, by_tokens) + grads
    return jax.shard_map(body, mesh=mesh, in_specs=in_specs, out_specs=out_specs, check_vma=False)
```

time: 1240 us -> 542 us (0.44)
  waiting for transfers between devices: 655 us -> 249 us
  matrix products: 241 us -> 90.6 us
  other arithmetic: 137 us -> 22.3 us
  blocking collectives: 85.4 us -> 0 us
  Pallas kernels: 0 us -> 63.8 us
    unnamed x16 -> x2, waiting for transfers between devices: 359 us -> 0.03 us
    all_gather x10 -> x1, waiting for transfers between devices: 296 us -> 43 us  [body(): gathered = lax.all_gather(packed, ('dp', 'ctx'), axis=0, tiled=False)]
    dot_general x24 -> x6, matrix products: 180 us -> 36 us  [product(): return jnp.dot(left_side, right_side, preferred_element_type=WIDE)]
    reduce_scatter x4 -> x1, waiting for transfers between devices: 0.01 us -> 126 us  [body(): lax.psum_scatter(packed_terms, ('dp', 'ctx'), scatter_dimension=0, tiled=...]
    all_gather x6 -> x0, other arithmetic: 91.2 us -> none  [gather_params(): lax.all_gather(as_sent(flats), ('dp', 'ctx'), axis=0, tiled=True)]
    unnamed x2 -> x0, blocking collectives: 85.4 us -> none
    ppermute x0 -> x4, waiting for transfers between devices: none -> 79.4 us  [the longest x2 54.3 us: swap_in(): lax.ppermute(piece, 'ctx', [(i, (i + shift) % ranks) for i in range(ranks)])]
    pallas_call x0 -> x2, Pallas kernels: none -> 63.8 us  [the longest x1 32.4 us: attend(): pl.pallas_call(functools.partial(attend_kernel, block), grid_spec=pltpu.P...]
  transfers between devices with their start and end apart: 15 -> 6, of which waited for: 11 -> 4; matrix products, arithmetic and copies ran while one was open for 27% -> 8% of each run, Pallas kernels for 0% -> 0%
where the time goes in v1:
time: 542 us; the launch traced here: 537 us
  waiting for transfers between devices  249 us (46%)
  local copies, waits for them, and re-layouts  91.2 us (17%)
  matrix products  90.6 us (17%)
  Pallas kernels  63.8 us (12%)
  other arithmetic  22.3 us (4%)
  between operations  15 us (3%)
    reduce_scatter x1, waiting for transfers between devices, body(): lax.psum_scatter(packed_terms, ('dp', 'ctx'), scatter_dimension=0, tiled=...  126 us
    ppermute x2, waiting for transfers between devices, swap_in(): lax.ppermute(piece, 'ctx', [(i, (i + shift) % ranks) for i in range(ranks)])  54.3 us
    all_gather x1, waiting for transfers between devices, body(): gathered = lax.all_gather(packed, ('dp', 'ctx'), axis=0, tiled=False)  43 us
    dot_general x6, matrix products, product(): return jnp.dot(left_side, right_side, preferred_element_type=WIDE)  36 us
    pallas_call x1, Pallas kernels, attend(): pl.pallas_call(functools.partial(attend_kernel, block), grid_spec=pltpu.P...  32.4 us
    pallas_call x1, Pallas kernels, attend_back(): pl.pallas_call(functools.partial(attend_back_kernel, block), grid_spec=pl...  31.4 us
    dot_general x6, matrix products, transposed_times(): lax.dot_general(left_side, right_side, (((0,), (0,)), ((), ())), preferre...  28.5 us
    unnamed x114, local copies, waits for them, and re-layouts  27.1 us
  transfers between devices with their start and end apart: 6, of which 4 were waited for; matrix products, arithmetic and copies ran while one was open for 8% of the time, Pallas kernels for 0%

profile of v1, /device:TPU:0, one launch (start us, length us, event | category | flops | bytes accessed | tf_op | source)
XLA Modules:
  0.0 537.0 jit_solution(7006363893058696509)
XLA Ops:
  13.4 6.1 %concatenate.18 = bf16[288]{0:T(512)(128)(2,1)S(1)} concatenate(bf16[24]{0:T(256)(128)(2,1)} %param.27, bf16[24]{0:T(256)(128)(2,1)} %param.28, bf16[24]{0:T(256)(128)(2,1)} %param.29, bf16[24]{0:T(256)(128)(2,1)} %param.30, bf16[24]{0:T(256)(128)(2,1)} %param.31, bf16[96]{0:T(256)(128)(2,1)} %param.32, bf16[24]{0:T(256)(128)(2,1)} %param.33, bf16[24]{0:T(256)(128)(2,1)} %param.34, ...), dimensions={0} | concatenate | bytes 1152 | tf_op jit(solution)/shard_map/gather/concatenate | solution.py:304
  21.4 2.1 constant_dynamic-slice_fusion.2
  23.5 1.6 copy.93
  25.1 3.0 collective-permute-start.2
  28.1 1.5 constant_dynamic-slice_fusion.7
  29.5 1.2 copy.92
  32.4 1.2 copy.73
  34.8 1.4 broadcast_in_dim.13
  36.2 2.1 bitcast_dynamic-update-slice_fusion.5
  38.3 2.1 broadcast_in_dim.17
  40.3 1.3 bitcast_dynamic-update-slice_fusion.1
  41.6 54.3 %collective-permute-done = bf16[1,512,768]{1,2,0:T(8,128)(2,1)} collective-permute-done((bf16[1,512,768]{1,2,0:T(8,128)(2,1)}, bf16[1,512,768]{1,2,0:T(8,128)(2,1)}, u32[]{:S(2)}, u32[]{:S(2)}) %collective-permute-start) | collective-permute-done | bytes 786464 | tf_op jit(solution)/shard_map/swap_in/ppermute | solution.py:276
  95.9 2.1 bitcast_dynamic-update-slice_fusion.4
  98.0 3.1 bitcast_dynamic-update-slice_fusion
  101.1 43.0 %all-gather.3.cloned.1.call-done = bf16[9472,768]{1,0:T(8,128)(2,1)} async-done(((bf16[296,768]{1,0:T(8,128)(2,1)}), bf16[9472,768]{1,0:T(8,128)(2,1)}) %all-gather.3.cloned.1.call-update) | async-done | bytes 14549008 | tf_op jit(solution)/shard_map/gather/all_gather | solution.py:342
  144.2 6.9 %fusion.57 = (bf16[32,24,768]{2,1,0:T(8,128)(2,1)S(1)}, bf16[32,24,768]{2,1,0:T(8,128)(2,1)}, bf16[32,24,768]{2,1,0:T(8,128)(2,1)}, bf16[32,24,768]{2,1,0:T(8,12...) fusion(bf16[32,296,768]{2,1,0:T(8,128)(2,1)} %bitcast.139), kind=kLoop, calls=%fused_computation.154 | loop fusion | bytes 18874368 | tf_op jit(solution)/shard_map/gather/slice | solution.py:320
  151.1 1.3 slice.232
  153.9 4.9 slice.246
  161.2 4.0 fusion.41.k_ref
  165.3 4.1 fusion.43.q_ref
  169.3 4.0 fusion.44.v_ref
  174.4 32.4 %attend.1 = (f32[1,1024,768]{2,1,0:T(8,128)}, bf16[1,1024,768]{2,1,0:T(8,128)(2,1)}, f32[1,6,2,1024]{3,2,1,0:T(2,128)}) custom-call(s32[8]{0:T(128)} %reshape.669.ranges, bf16[1,1024,768]{2,1,0:T(8,128)(2,1)} %fusion.43.q_ref, bf16[1,1024,768]{2,1,0:T(8,128)(2,1)} %fusion.41.k_ref, bf16[1,1024,768]{2,1,0:T(8,128)(2,1)} %fusion.44.v_ref, ...), custom_call_target="tpu_custom_call" | custom-call | tf_op jit(solution)/shard_map/forward/attend/pallas_call | solution.py:219
  206.8 3.8 fusion.59
  211.7 3.5 pad_maximum_fusion
  215.2 10.2 %multiply_convert_fusion = (bf16[1024,3072]{1,0:T(8,128)(2,1)S(1)}, f32[1024,3072]{1,0:T(8,128)}) fusion(f32[3072]{0:T(1024)S(1)} %reshape.703, bf16[768,3072]{1,0:T(8,128)(2,1)S(1)} %bitcast.159, f32[1024,768]{0,1:T(8,128)S(1)} %get-tuple-element.91, f32[768]{0:T(1024)S(1)} %reshape.702, f32[768]{0:T(1024)S(1)} %reshape.701, f32[1024]{0:T(1024)S(1)} %add_rsqrt_fusion.1, ...), kind=kOutput, calls=%fused_computation.6 | convolution fusion | flops 4854644736 | bytes 26765312 | tf_op jit(solution)/shard_map/forward/dot_general | solution.py:23
  225.4 9.9 %fusion.60 = (f32[1024]{0:T(1024)S(1)}, f32[1024,768]{0,1:T(8,128)S(1)}) fusion(f32[768]{0:T(1024)S(1)} %reshape.704, bf16[1024,3072]{1,0:T(8,128)(2,1)S(1)} %get-tuple-element.92, bf16[3072,768]{1,0:T(8,128)(2,1)S(1)} %bitcast.152, f32[768]{0:T(1024)S(1)} %reshape.702, f32[768]{0:T(1024)S(1)} %reshape.701, f32[1024]{0:T(1024)S(1)} %add_rsqrt_fusion.1, ...), kind=kOutput, calls=%fused_computation.157 | convolution fusion | flops 4837342208 | bytes 17323008 | tf_op jit(solution)/shard_map/forward/dot_general | solution.py:23
  236.3 3.2 multiply_reduce_fusion
  239.5 4.9 fusion.54
  244.4 13.1 %fusion.61 = (bf16[3072]{0:T(1024)(128)(2,1)S(1)}, bf16[1024,3072]{1,0:T(8,128)(2,1)S(1)}) fusion(f32[1024,3072]{1,0:T(8,128)} %get-tuple-element.93, f32[3072]{0:T(1024)S(1)} %reshape.703, bf16[3072,768]{1,0:T(8,128)(2,1)S(1)} %bitcast.155, f32[1024,768]{0,1:T(8,128)S(1)} %get-tuple-element.42), kind=kOutput, calls=%fused_computation.158 | convolution fusion | flops 4870370304 | bytes 26757120 | tf_op jit(solution)/shard_map/backward/dot_general | solution.py:27
  257.6 6.0 %multiply_reduce_fusion.1 = (bf16[768]{0:T(1024)(128)(2,1)S(1)}, f32[1024]{0:T(1024)S(1)}, f32[1024]{0:T(1024)S(1)}, bf16[768]{0:T(1024)(128)(2,1)S(1)}, f32[1024,768]{0,1:T(8,128)S(1)}) fusion(f32[1024,768]{0,1:T(8,128)S(1)} %copy-done.1, f32[1024]{0:T(1024)S(1)} %add_rsqrt_fusion.1, f32[1024]{0:T(1024)S(1)} %broadcast_multiply_fusion.5, ...), kind=kOutput, calls=%fused_computation.12 | convolution fusion | flops 4839698432 | bytes 20469760 | tf_op jit(solution)/shard_map/backward/dot_general | solution.py:27
  263.6 7.2 %convolution_convert_fusion.1 = bf16[768,3072]{1,0:T(8,128)(2,1)} fusion(bf16[1024,3072]{1,0:T(8,128)(2,1)S(1)} %get-tuple-element.98, f32[1024,768]{0,1:T(8,128)S(1)} %copy-done.1, f32[768]{0:T(1024)S(1)} %reshape.702, f32[768]{0:T(1024)S(1)} %reshape.701, f32[1024]{0:T(1024)S(1)} %add_rsqrt_fusion.1, f32[1024]{0:T(1024)S(1)} %broadcast_multiply_fusion.5), kind=kOutput, calls=%fused_computation.9 | convolution fusion | flops 4838129664 | bytes 14170112 | tf_op jit(solution)/shard_map/backward/dot_general | solution.py:33
  270.9 1.2 fusion.55
  272.1 2.7 fusion.42.g_ref
  274.8 31.4 %attend_back.1 = (bf16[1,1024,768]{2,1,0:T(8,128)(2,1)}, bf16[1,1024,768]{2,1,0:T(8,128)(2,1)}, bf16[1,1024,768]{2,1,0:T(8,128)(2,1)}) custom-call(s32[8]{0:T(128)} %reshape.669.ranges, bf16[1,1024,768]{2,1,0:T(8,128)(2,1)} %fusion.43.q_ref, bf16[1,1024,768]{2,1,0:T(8,128)(2,1)} %fusion.41.k_ref, bf16[1,1024,768]{2,1,0:T(8,128)(2,1)} %fusion.44.v_ref, ...), custom_call_target="tpu_custom_call" | custom-call | tf_op jit(solution)/shard_map/backward/attend_back/pallas_call | solution.py:242
  306.2 1.7 reduce_sum.193
  307.9 4.3 fusion.30
  312.2 1.7 reduce_sum.194
  313.9 4.5 fusion.36
  318.4 2.5 fusion.27
  321.1 7.0 %convolution_convert_fusion = bf16[3072,768]{1,0:T(8,128)(2,1)} fusion(bf16[1024,3072]{1,0:T(8,128)(2,1)S(1)} %bitcast.184, f32[1024,768]{0,1:T(8,128)S(1)} %copy-done.11), kind=kOutput, calls=%fused_computation.8 | convolution fusion | flops 4834983936 | bytes 14155776 | tf_op jit(solution)/shard_map/backward/dot_general | solution.py:33
  329.2 1.2 constant_dynamic-update-slice_fusion.15
  330.4 2.9 fusion.33
  333.4 1.2 constant_dynamic-update-slice_fusion.14
  337.2 1.2 slice_dynamic-update-slice_fusion.3
  338.4 1.2 slice_dynamic-update-slice_fusion.2
  339.6 1.2 slice_dynamic-update-slice_fusion.1
  340.8 1.2 slice_dynamic-update-slice_fusion
  342.0 2.5 constant_dynamic-update-slice_fusion.11
  345.3 1.9 copy-done.2
  347.1 2.0 constant_dynamic-slice_fusion.4
  349.2 3.2 copy.78
  352.3 1.4 collective-permute-start.1
  353.8 1.4 fusion.21
  355.2 1.4 fusion.17
  357.9 1.4 add_convert_fusion
  359.5 1.2 copy.86
  363.1 1.2 bitcast_dynamic-update-slice_fusion.3
  364.3 1.9 broadcast_in_dim.12
  366.1 1.2 bitcast_dynamic-update-slice_fusion.2
  367.4 25.1 %collective-permute-done.3 = bf16[1,512,768]{2,1,0:T(8,128)(2,1)} collective-permute-done((bf16[1,512,768]{2,1,0:T(8,128)(2,1)}, bf16[1,512,768]{2,1,0:T(8,128)(2,1)}, u32[]{:S(2)}, u32[]{:S(2)}) %collective-permute-start.3) | collective-permute-done | bytes 786464 | tf_op jit(solution)/shard_map/swap_out/ppermute | solution.py:289
  392.5 1.2 constant_dynamic-update-slice_fusion.16
  393.7 1.9 convert_element_type.259
  395.6 2.8 constant_dynamic-update-slice_fusion.17
  398.4 126.4 %reduce-scatter.2.cloned.1.call-done = bf16[1,296,768]{2,1,0:T(8,128)(2,1)} async-done(((bf16[32,296,768]{2,1,0:T(8,128)(2,1)}), bf16[1,296,768]{2,1,0:T(8,128)(2,1)}) %reduce-scatter.2.cloned.1.call-update) | async-done | bytes 454672 | tf_op jit(solution)/shard_map/scatter/reduce_scatter | solution.py:461
  (176 shorter events, 31.4 us)
Async XLA Ops:
  7.2 137.0 %all-gather.3.cloned.1.call-start = ((), (), s32[]{:S(2)}) async-start(), calls=%async_computation.2 | async-start | bytes 15003648 | tf_op jit(solution)/shard_map/gather/all_gather | solution.py:342
  20.5 0.8 copy-start.21
  21.3 503.4 %reduce-scatter.2.cloned.1.call-start = ((), (), s32[]{:S(2)}) async-start(), calls=%async_computation.1 | async-start | bytes 15003648 | tf_op jit(solution)/shard_map/scatter/reduce_scatter | solution.py:461
  25.1 6.2 %copy-start.29 = (s32[2,1024]{1,0:T(2,128)S(1)}, s32[2,1024]{1,0:T(2,128)}, u32[]{:S(2)}) copy-start(s32[2,1024]{1,0:T(2,128)} %param.19) | copy-start | bytes 24580
  25.1 72.9 %collective-permute-start.2 = (f32[1,512,768]{1,2,0:T(8,128)}, f32[1,512,768]{1,2,0:T(8,128)}, u32[]{:S(2)}, u32[]{:S(2)}) collective-permute-start(f32[1,512,768]{1,2,0:T(8,128)} %copy.93), channel_id=1, source_target_pairs={{0,1},{1,0},{2,3},{3,2},{4,5},{5,4},{6,7},{7,6},{8,9},{9,8},{10,11... | collective-permute-start | bytes 4718600 | tf_op jit(solution)/shard_map/swap_in/ppermute | solution.py:276
  30.7 65.1 %collective-permute-start = (bf16[1,512,768]{1,2,0:T(8,128)(2,1)}, bf16[1,512,768]{1,2,0:T(8,128)(2,1)}, u32[]{:S(2)}, u32[]{:S(2)}) collective-permute-start(bf16[1,512,768]{1,2,0:T(8,128)(2,1)} %copy.92), channel_id=1, source_target_pairs={{0,1},{1,0},{2,3},{3,2},{4,5},{5,4},{6,7},{7,6},{8,9},{9,8},{10,11... | collective-permute-start | bytes 2359304 | tf_op jit(solution)/shard_map/swap_in/ppermute | solution.py:276
  31.9 141.4 %copy-start.22 = (s32[1,1024]{1,0:T(1,128)}, s32[1,1024]{1,0:T(1,128)S(1)}, u32[]{:S(2)}) copy-start(s32[1,1024]{1,0:T(1,128)S(1)} %get-tuple-element.46) | copy-start | bytes 12292
  151.1 10.1 %copy-start.13 = (bf16[32,24,768]{2,1,0:T(8,128)(2,1)}, bf16[32,24,768]{2,1,0:T(8,128)(2,1)S(1)}, u32[]{:S(2)}) copy-start(bf16[32,24,768]{2,1,0:T(8,128)(2,1)S(1)} %get-tuple-element.53) | copy-start | bytes 3538948
  151.1 14.2 %copy-start.15 = (bf16[32,24,768]{2,1,0:T(8,128)(2,1)}, bf16[32,24,768]{2,1,0:T(8,128)(2,1)S(1)}, u32[]{:S(2)}) copy-start(bf16[32,24,768]{2,1,0:T(8,128)(2,1)S(1)} %get-tuple-element.54) | copy-start | bytes 3538948
  151.1 18.2 %copy-start.7 = (bf16[32,24,768]{2,1,0:T(8,128)(2,1)}, bf16[32,24,768]{2,1,0:T(8,128)(2,1)S(1)}, u32[]{:S(2)}) copy-start(bf16[32,24,768]{2,1,0:T(8,128)(2,1)S(1)} %get-tuple-element.47) | copy-start | bytes 3538948
  210.6 4.6 copy-start
  210.6 0.7 copy-start.27
  210.6 0.8 copy-start.26
  210.6 0.9 copy-start.28
  210.6 1.0 copy-start.25
  211.7 13.7 %slice-start.2 = ((s8[4718592]{0:T(1024)(128)(4,1)}), s8[4194304]{0:T(1024)(128)(4,1)S(1)}, s32[]{:S(2)}) async-start(s8[4718592]{0:T(1024)(128)(4,1)} %bitcast.150), calls=%async_computation.5 | async-start | bytes 8388608
  215.2 10.2 %copy-start.9 = (bf16[32,24,3072]{2,1,0:T(8,128)(2,1)}, bf16[32,24,3072]{2,1,0:T(8,128)(2,1)S(1)}, u32[]{:S(2)}) copy-start(bf16[32,24,3072]{2,1,0:T(8,128)(2,1)S(1)} %pad_maximum_fusion) | copy-start | bytes 14155780
  215.2 10.2 %slice-start.3 = ((s8[4718592]{0:T(1024)(128)(4,1)}), s8[524288]{0:T(1024)(128)(4,1)S(1)}, s32[]{:S(2)}) async-start(s8[4718592]{0:T(1024)(128)(4,1)} %bitcast.150), calls=%async_computation.6 | async-start | bytes 1048576
  225.4 10.0 %copy-start.33 = (bf16[1024,3072]{1,0:T(8,128)(2,1)}, bf16[1024,3072]{1,0:T(8,128)(2,1)S(1)}, u32[]{:S(2)}) copy-start(bf16[1024,3072]{1,0:T(8,128)(2,1)S(1)} %get-tuple-element.92) | copy-start | bytes 18874372
  235.4 0.7 copy-start.24
  235.4 0.8 copy-start.23
  236.3 8.1 %slice-start.4 = ((s8[4718592]{0:T(1024)(128)(4,1)}), s8[4194304]{0:T(1024)(128)(4,1)S(1)}, s32[]{:S(2)}) async-start(s8[4718592]{0:T(1024)(128)(4,1)} %bitcast.153), calls=%async_computation.7 | async-start | bytes 8388608
  239.5 4.9 slice-start.5
  239.5 18.1 %slice-start.8 = ((s8[4718592]{0:T(1024)(128)(4,1)}), s8[4194304]{0:T(1024)(128)(4,1)S(1)}, s32[]{:S(2)}) async-start(s8[4718592]{0:T(1024)(128)(4,1)} %bitcast.160), calls=%async_computation.11 | async-start | bytes 8388608
  244.4 13.2 %copy-start.10 = (f32[1024,768]{0,1:T(8,128)}, f32[1024,768]{0,1:T(8,128)S(1)}, u32[]{:S(2)}) copy-start(f32[1024,768]{0,1:T(8,128)S(1)} %get-tuple-element.42) | copy-start | bytes 9437188
  244.4 13.2 %copy-start.1 = (f32[1024,768]{0,1:T(8,128)S(1)}, f32[1024,768]{0,1:T(8,128)}, u32[]{:S(2)}) copy-start(f32[1024,768]{0,1:T(8,128)} %copy-done) | copy-start | bytes 9437188
  244.4 13.2 %slice-start.9 = ((s8[4718592]{0:T(1024)(128)(4,1)}), s8[524288]{0:T(1024)(128)(4,1)S(1)}, s32[]{:S(2)}) async-start(s8[4718592]{0:T(1024)(128)(4,1)} %bitcast.160), calls=%async_computation.12 | async-start | bytes 1048576
  270.8 1.3 copy-start.17
  272.0 46.4 %copy-start.3 = (f32[1024,768]{0,1:T(8,128)}, f32[1024,768]{0,1:T(8,128)S(1)}, u32[]{:S(2)}) copy-start(f32[1024,768]{0,1:T(8,128)S(1)} %get-tuple-element.44) | copy-start | bytes 9437188
  313.9 4.5 copy-start.32
  313.9 7.1 %slice-start.10 = ((s8[6291456]{0:T(1024)(128)(4,1)}), s8[4194304]{0:T(1024)(128)(4,1)S(1)}, s32[]{:S(2)}) async-start(s8[6291456]{0:T(1024)(128)(4,1)} %bitcast.183), calls=%async_computation.13 | async-start | bytes 8388608
  318.4 2.6 copy-start.11
  318.4 2.6 slice-start.11
  321.1 8.2 %copy-start.20 = (bf16[768,768]{1,0:T(8,128)(2,1)S(1)}, bf16[768,768]{1,0:T(8,128)(2,1)}, u32[]{:S(2)}) copy-start(bf16[768,768]{1,0:T(8,128)(2,1)} %fusion.30) | copy-start | bytes 3538948
  328.1 2.3 copy-start.30
  330.4 6.9 %slice-start = ((s8[4718592]{0:T(1024)(128)(4,1)}), s8[4194304]{0:T(1024)(128)(4,1)S(1)}, s32[]{:S(2)}) async-start(s8[4718592]{0:T(1024)(128)(4,1)} %bitcast.144), calls=%async_computation.3 | async-start | bytes 8388608
  330.4 6.9 %slice-start.1 = ((s8[4718592]{0:T(1024)(128)(4,1)}), s8[524288]{0:T(1024)(128)(4,1)S(1)}, s32[]{:S(2)}) async-start(s8[4718592]{0:T(1024)(128)(4,1)} %bitcast.144), calls=%async_computation.4 | async-start | bytes 1048576
  333.3 1.7 copy-start.19
  333.3 2.8 copy-start.18
  335.0 6.9 %slice-start.6 = ((s8[4718592]{0:T(1024)(128)(4,1)}), s8[4194304]{0:T(1024)(128)(4,1)S(1)}, s32[]{:S(2)}) async-start(s8[4718592]{0:T(1024)(128)(4,1)} %bitcast.156), calls=%async_computation.9 | async-start | bytes 8388608
  337.2 4.7 slice-start.7
  345.2 1.9 copy-start.2
  349.2 4.6 copy-start.12
  349.2 4.6 copy-start.16
  352.3 2.9 copy-start.14
  352.3 2.9 copy-start.31
  352.3 43.3 %collective-permute-start.1 = (f32[1,512,768]{2,1,0:T(8,128)}, f32[1,512,768]{2,1,0:T(8,128)}, u32[]{:S(2)}, u32[]{:S(2)}) collective-permute-start(f32[1,512,768]{2,1,0:T(8,128)} %bitcast.18), channel_id=1, source_target_pairs={{0,1},{1,0},{2,3},{3,2},{4,5},{5,4},{6,7},{7,6},{8,9},{9,8},{10,11... | collective-permute-start | bytes 4718600 | tf_op jit(solution)/shard_map/swap_out/ppermute | solution.py:289
  355.2 1.9 copy-start.4
  355.2 2.3 copy-start.5
  355.2 2.7 copy-start.8
  359.3 3.1 copy-start.6
  360.7 31.7 %collective-permute-start.3 = (bf16[1,512,768]{2,1,0:T(8,128)(2,1)}, bf16[1,512,768]{2,1,0:T(8,128)(2,1)}, u32[]{:S(2)}, u32[]{:S(2)}) collective-permute-start(bf16[1,512,768]{2,1,0:T(8,128)(2,1)} %bitcast.176), channel_id=1, source_target_pairs={{0,1},{1,0},{2,3},{3,2},{4,5},{5,4},{6,7},{7,6},{8,9},{9,8},{10,11... | collective-permute-start | bytes 2359304 | tf_op jit(solution)/shard_map/swap_out/ppermute | solution.py:289
Sparse Core Ops, SparseCore 0:
  21.4 122.6 all-gather.2
  345.4 179.3 reduce-scatter.1
